TPU v7x, 32 devices: a whole 2x2x4 slice. The times are simulated.
32 devices in a mesh: freq: 8 (over y, x, core), rcv: 4 (over z).
Axes of the slice: x: 2, y: 2, z: 4, core: 2. Of those that a mesh axis runs over, the one named last changes fastest.
Arguments:
- green_freq: float32 [2, 8, 2304, 2304], P(None, 'freq', 'rcv'), may hold values from -6 to 6
- data_matrix: float32 [2, 8, 2304, 2304], P(None, 'freq', 'rcv'), may hold values from -0.09375 to 0.09375
- shot_panels: float32 [2, 8, 2304, 256], P(None, 'freq', 'rcv'), may hold values from -6 to 6
- wavelet: float32 [2, 8], P(None, 'freq'), may hold values from -1.5 to 1.5
- sources: int32 [256], replicated, may hold values from 0 to 2303, as said below
- support: int32 [8, 2304], replicated, may hold values 0 or 1
- threshold: float32 [1], replicated, may hold values from 3 to 7
Outputs:
- green_next: float32 [2, 8, 2304, 2304], P(None, 'freq', 'rcv')
- residual: float32 [2, 8, 2304, 256], P(None, 'freq', 'rcv')
Inputs may be any that keep to these rules, and one draw needn't show every extreme that they name: `sources`: 256 distinct source positions. `support`: a 0/1 mask over time samples and source positions.
All inputs are finite; a program needn't handle non-finite values.
Results may differ from a plain program's by a relative error of at most 0.00013.
Values sent between devices are 32-bit elements; how exact they have to be, the bound alone decides.
A program may use at most 128 MiB of HBM per device.

v0:
```python
import math
import jax
import jax.numpy as jnp
from jax import lax
from jax.sharding import PartitionSpec as P

HIGHEST = lax.Precision.HIGHEST


def complex_product(left_pair, right_pair, pattern):
    left_real, left_imag = left_pair
    right_real, right_imag = right_pair
    real_part = jnp.einsum(pattern, left_real, right_real, precision=HIGHEST) - jnp.einsum(
        pattern, left_imag, right_imag, precision=HIGHEST
    )
    imag_part = jnp.einsum(pattern, left_real, right_imag, precision=HIGHEST) + jnp.einsum(
        pattern, left_imag, right_real, precision=HIGHEST
    )
    return (real_part, imag_part)


def conj_product(left_pair, right_pair, pattern):
    left_real, left_imag = left_pair
    right_real, right_imag = right_pair
    real_part = jnp.einsum(pattern, left_real, right_real, precision=HIGHEST) + jnp.einsum(
        pattern, left_imag, right_imag, precision=HIGHEST
    )
    imag_part = jnp.einsum(pattern, left_real, right_imag, precision=HIGHEST) - jnp.einsum(
        pattern, left_imag, right_real, precision=HIGHEST
    )
    return (real_part, imag_part)


def shrink_spectra(spectra, keep, shrink_level):
    n_freq = spectra.shape[1]
    grid = jnp.arange(n_freq, dtype=jnp.int32)
    phase = grid[:, None] * grid[None, :] % n_freq
    angle = phase.astype(jnp.float32) * (2.0 * math.pi / n_freq)
    cos_table = jnp.cos(angle)
    sin_table = jnp.sin(angle)
    pattern = "tf,f...->t..."
    time_real = jnp.einsum(pattern, cos_table, spectra[0], precision=HIGHEST) - jnp.einsum(
        pattern, sin_table, spectra[1], precision=HIGHEST
    )
    time_imag = jnp.einsum(pattern, sin_table, spectra[0], precision=HIGHEST) + jnp.einsum(
        pattern, cos_table, spectra[1], precision=HIGHEST
    )
    magnitude = jnp.sqrt(time_real * time_real + time_imag * time_imag)
    factor = (
        jnp.maximum(magnitude - shrink_level, 0.0) / jnp.maximum(magnitude, shrink_level) * keep
    )
    kept_real = factor * time_real
    kept_imag = factor * time_imag
    back_real = (
        jnp.einsum(pattern, cos_table, kept_real, precision=HIGHEST)
        + jnp.einsum(pattern, sin_table, kept_imag, precision=HIGHEST)
    ) / n_freq
    back_imag = (
        jnp.einsum(pattern, cos_table, kept_imag, precision=HIGHEST)
        - jnp.einsum(pattern, sin_table, kept_real, precision=HIGHEST)
    ) / n_freq
    return jnp.stack([back_real, back_imag])


def on_device(green_freq, data_matrix, shot_panels, wavelet, sources, support, threshold):
    data_pair = (data_matrix[0], data_matrix[1])
    picked = jnp.take(green_freq, sources, axis=3)
    wave_real = wavelet[0][:, None, None]
    wave_imag = wavelet[1][:, None, None]
    rows_here = green_freq.shape[2]
    shard_piece = lax.all_gather(picked, "rcv", axis=2, tiled=True)
    block_real = data_matrix[0]
    block_imag = data_matrix[1]
    real_part, imag_part = complex_product(
        (block_real, block_imag), (shard_piece[0], shard_piece[1]), "frk,fkc->frc"
    )
    multiple = jnp.stack([real_part, imag_part])
    resid_real = shot_panels[0] - (wave_real * picked[0] - wave_imag * picked[1] - multiple[0])
    resid_imag = shot_panels[1] - (wave_real * picked[1] + wave_imag * picked[0] - multiple[1])
    residual = jnp.stack([resid_real, resid_imag])
    local_real = wave_real * resid_real + wave_imag * resid_imag
    local_imag = wave_real * resid_imag - wave_imag * resid_real
    adj_real, adj_imag = conj_product(data_pair, (resid_real, resid_imag), "frk,frc->kfc")
    summed_terms = -jnp.stack([adj_real, adj_imag], axis=1)
    own_rows = jnp.transpose(jnp.stack([local_real, local_imag]), (2, 0, 1, 3))
    row_offset = lax.axis_index("rcv") * rows_here
    summed_terms = summed_terms + lax.dynamic_update_slice_in_dim(
        jnp.zeros_like(summed_terms), own_rows, row_offset, 0
    )
    summed_all = lax.psum(summed_terms, "rcv")
    mine = lax.dynamic_slice_in_dim(summed_all, row_offset, rows_here, 0)
    direction = jnp.transpose(mine, (1, 2, 0, 3))
    push_real, push_imag = complex_product(
        data_pair, (summed_all[:, 0], summed_all[:, 1]), "frk,kfc->frc"
    )
    pushed = jnp.stack([push_real, push_imag])
    image_real = wave_real * direction[0] - wave_imag * direction[1] - pushed[0]
    image_imag = wave_real * direction[1] + wave_imag * direction[0] - pushed[1]
    norm_dir = jnp.sum(direction * direction)
    norm_img = jnp.sum(image_real * image_real + image_imag * image_imag)
    totals = lax.psum((norm_dir, norm_img), ("freq", "rcv"))
    step_size = totals[0] / totals[1]
    updated = green_freq.at[:, :, :, sources].add(step_size * direction)
    keep_all = support.astype(jnp.float32)
    gathered = lax.all_to_all(updated, "freq", split_axis=2, concat_axis=1, tiled=True)
    shrunk = shrink_spectra(gathered, keep_all[:, None, :], threshold[0])
    green_next = lax.all_to_all(shrunk, "freq", split_axis=1, concat_axis=2, tiled=True)
    return (green_next, residual)


def solution(mesh):
    in_specs = (
        P(None, "freq", "rcv", None),
        P(None, "freq", "rcv", None),
        P(None, "freq", "rcv", None),
        P(None, "freq"),
        P(),
        P(),
        P(),
    )
    out_specs = (P(None, "freq", "rcv", None), P(None, "freq", "rcv", None))
    return jax.shard_map(
        on_device, mesh=mesh, in_specs=in_specs, out_specs=out_specs, check_vma=False
    )
```

profile of v0, /device:TPU:0, one launch (start us, length us, event | category | flops | bytes accessed | tf_op | source)
XLA Modules:
  0.0 851.4 jit_solution(611839117997585425)
XLA Ops:
  7.2 0.0 all-gather.2.cloned.1.call-start
  7.2 0.7 compare_select_fusion
  7.9 0.7 compare_and_fusion
  8.6 19.2 %copy.30 = f32[2,1,576,2304]{2,0,3,1:T(2,128)} copy(f32[2,1,576,2304]{3,2,1,0:T(8,128)} %param.7) | data formatting | bytes 21233664 | tf_op args[0]
  27.8 6.5 gather_fusion
  34.4 1.2 copy.31
  35.6 1.1 bitcast_select_fusion
  36.7 0.0 all-gather.2.cloned.1.call-update
  36.8 0.3 all-reduce.3.cloned.1.call-start
  37.1 0.7 fusion.175
  37.8 91.2 %all-gather.2.cloned.1.call-done = f32[2,1,2304,256]{3,2,1,0:T(8,128)} async-done(((f32[2,1,576,256]{3,2,1,0:T(8,128)}), f32[2,1,2304,256]{3,2,1,0:T(8,128)}) %all-gather.2.cloned.1.call-update) | async-done | bytes 4718608 | tf_op jit(solution)/shard_map/all_gather | solution.py:71
  129.0 7.5 fusion.8
  136.5 0.0 slice-start.1
  136.5 0.0 slice-start.2
  136.5 0.0 slice-start.7
  136.6 9.7 %fusion.101 = f32[576,256]{1,0:T(8,128)S(1)} fusion(f32[256,576]{0,1:T(8,128)S(1)} %fusion.8, f32[2,1,576,2304]{3,2,1,0:T(8,128)} %param.8, f32[2,1,2304,256]{3,2,1,0:T(8,128)} %all-gather.2.cloned.1.call-done, f32[2,1,576,256]{3,2,1,0:T(8,128)} %param.9, f32[2,1,576,256]{3,2,1,0:T(8,128)S(1)} %copy-done.2, f32[]{:T(128)} %bitcast.6, f32[]{:T(128)} %bitcast.3), kind=kOutput, calls=%fused_computation.76 | convolution fusion | flops 4077748224 | bytes 10617856 | tf_op jit(solution)/shard_map/frk,fkc->frc/dot_general | solution.py:16
  146.3 11.9 %fusion.6 = f32[256,2304]{0,1:T(8,128)S(1)} fusion(f32[576,256]{1,0:T(8,128)S(1)} %fusion.101, f32[2,1,576,2304]{3,2,1,0:T(8,128)} %param.8), kind=kOutput, calls=%fused_computation.9 | convolution fusion | flops 4076863488 | bytes 8257536 | tf_op jit(solution)/shard_map/frk,frc->kfc/dot_general | solution.py:25
  158.2 0.0 slice-done
  158.2 0.0 slice-done.6
  158.2 0.0 slice-done.1
  158.2 0.0 slice-done.2
  158.2 0.0 slice-done.7
  158.2 0.0 copy-start.3
  158.3 4.4 fusion.10
  162.6 5.7 fusion.98
  168.3 9.6 %fusion.4 = f32[256,2304]{0,1:T(8,128)S(1)} fusion(f32[576,256]{1,0:T(8,128)S(1)} %fusion.98, f32[2,1,576,2304]{3,2,1,0:T(8,128)S(1)} %bitcast.238), kind=kOutput, calls=%fused_computation.7 | convolution fusion | flops 4076863488 | bytes 8257536 | tf_op jit(solution)/shard_map/frk,frc->kfc/dot_general | solution.py:28
  177.9 1.4 add_bitcast_fusion
  179.3 9.7 %fusion.41 = f32[2304,1,1,256]{3,0,2,1:T(8,128)S(1)} fusion(f32[256,2304]{0,1:T(8,128)S(1)} %fusion.6, f32[576,256]{1,0:T(8,128)S(1)} %fusion.98, f32[2,1,576,2304]{3,2,1,0:T(8,128)S(1)} %bitcast.238), kind=kOutput, calls=%fused_computation.44 | convolution fusion | flops 4077453312 | bytes 10616832 | tf_op jit(solution)/shard_map/frk,frc->kfc/dot_general | solution.py:25
  189.0 9.9 %fusion.38 = f32[2304,1,1,256]{3,0,2,1:T(8,128)S(1)} fusion(f32[256,2304]{0,1:T(8,128)S(1)} %fusion.4, f32[576,256]{1,0:T(8,128)S(1)} %fusion.101, f32[2,1,576,2304]{3,2,1,0:T(8,128)S(1)} %bitcast.238), kind=kOutput, calls=%fused_computation.43 | convolution fusion | flops 4077453312 | bytes 10616832 | tf_op jit(solution)/shard_map/frk,frc->kfc/dot_general | solution.py:28
  198.9 2.5 maximum_negate_fusion
  201.4 2.4 fusion.108
  203.8 0.0 all-reduce.3.cloned.1.call-update
  203.8 170.5 %all-reduce.3.cloned.1.call-done = f32[2304,2,1,256]{3,0,2,1:T(8,128)} async-done(((f32[2304,2,1,256]{3,0,2,1:T(8,128)}), f32[2304,2,1,256]{3,0,2,1:T(8,128)}) %all-reduce.3.cloned.1.call-update) | async-done | bytes 4718608 | tf_op jit(solution)/shard_map/psum | solution.py:90
  374.4 2.3 multiply_reduce_fusion
  376.7 7.8 fusion
  384.5 0.0 slice-start.5
  384.5 7.0 fusion.2
  391.5 0.0 slice-done.3
  391.5 5.6 fusion.83
  397.2 6.3 fusion.109
  403.5 39.4 %all-reduce = (f32[]{:T(128)}, f32[]{:T(128)}) all-reduce(f32[]{:T(128)} %get-tuple-element.8, f32[]{:T(128)} %fusion.109), channel_id=1, replica_groups=mesh['freq'=8,'rcv'=4] {'freq','rcv'}, use_global_device_ids=true, to_apply=%region_2.3 | all-reduce | flops 2 | bytes 16 | tf_op jit(solution)/shard_map/psum | solution.py:101
  444.2 2.4 multiply_bitcast_fusion.2
  446.6 2.7 copy.36
  449.2 31.0 %scatter_fusion = f32[2,576,2304]{1,0,2:T(2,128)} fusion(f32[2,576,2304]{1,0,2:T(2,128)} %bitcast.242, s32[256]{0:T(256)S(1)} %compare_select_fusion, f32[256,2,576]{2,1,0:T(2,128)S(1)} %copy.36), kind=kCustom, calls=%fused_computation.1 | custom fusion | flops 294912 | bytes 3539968 | tf_op jit(solution)/shard_map/scatter-add | solution.py:103
  480.3 21.2 %copy.37 = f32[2,1,576,2304]{3,0,1,2:T(2,128)} copy(f32[2,1,576,2304]{2,0,3,1:T(2,128)} %bitcast.243) | data formatting | bytes 21233664 | tf_op jit(solution)/shard_map/scatter-add | solution.py:103
  501.5 5.3 all-to-all-start
  507.5 117.2 %all-to-all-done = f32[2,1,576,2304]{3,0,1,2:T(2,128)} async-done(((f32[2,1,576,2304]{3,0,1,2:T(2,128)}), f32[2,1,576,2304]{3,0,1,2:T(2,128)}, u32[]{:S(2)}, u32[]{:S(2)}) %all-to-all-start) | async-done | bytes 10616864 | tf_op jit(solution)/shard_map/all_to_all | solution.py:105
  624.7 12.6 %fusion.174 = (f32[1,1,576,2304]{3,0,1,2:T(1,128)S(1)}, f32[1,1,576,2304]{3,0,1,2:T(1,128)S(1)}) fusion(f32[2,1,576,2304]{3,0,1,2:T(2,128)} %all-to-all-done), kind=kLoop, calls=%fused_computation.145 | loop fusion | bytes 21233664 | tf_op jit(solution)/shard_map/slice | solution.py:43
  637.3 0.3 copy.51
  637.7 7.0 fusion.30
  644.7 7.0 fusion.28
  651.8 0.3 copy.52
  652.1 7.1 convolution_subtract_fusion
  659.2 7.4 convolution_add_fusion
  666.6 7.6 fusion.121
  674.3 8.0 fusion.119
  682.3 8.8 %multiply_bitcast_fusion.1 = f32[1,8,72,2304]{3,1,2,0:T(8,128)} fusion(f32[8,72,2304]{2,0,1:T(8,128)S(1)} %fusion.121, f32[8,72,2304]{2,0,1:T(8,128)S(1)} %convolution_add_fusion, f32[8,72,2304]{2,0,1:T(8,128)S(1)} %convolution_subtract_fusion, f32[8,2304]{1,0:T(8,128)S(1)} %convert_element_type.21, f32[]{:T(128)} %bitcast.234), kind=kOutput, calls=%fused_computation.28 | convolution fusion | flops 142001024 | bytes 21307396 | tf_op jit(solution)/shard_map/tf,f...->t.../dot_general | solution.py:56
  691.1 9.0 %multiply_bitcast_fusion = f32[1,8,72,2304]{3,1,2,0:T(8,128)} fusion(f32[8,72,2304]{2,0,1:T(8,128)S(1)} %fusion.119, f32[8,72,2304]{2,0,1:T(8,128)S(1)} %convolution_subtract_fusion, f32[8,72,2304]{2,0,1:T(8,128)S(1)} %convolution_add_fusion, f32[8,2304]{1,0:T(8,128)S(1)} %convert_element_type.21, f32[]{:T(128)} %bitcast.235), kind=kOutput, calls=%fused_computation.27 | convolution fusion | flops 142001024 | bytes 21307396 | tf_op jit(solution)/shard_map/tf,f...->t.../dot_general | solution.py:60
  700.1 4.8 pad_maximum_fusion
  704.9 7.4 copy.44
  712.2 5.2 all-to-all-start.1
  717.4 1.1 pad_maximum_fusion.1
  718.5 116.8 %all-to-all-done.1 = f32[2,8,72,2304]{3,2,0,1:T(8,128)} async-done(((f32[2,8,72,2304]{3,2,0,1:T(8,128)}), f32[2,8,72,2304]{3,2,0,1:T(8,128)}, u32[]{:S(2)}, u32[]{:S(2)}) %all-to-all-start.1) | async-done | bytes 10616864 | tf_op jit(solution)/shard_map/all_to_all | solution.py:107
  835.3 9.0 %copy.45 = f32[2,8,72,2304]{3,2,1,0:T(8,128)} copy(f32[2,8,72,2304]{3,2,0,1:T(8,128)} %all-to-all-done.1) | data formatting | bytes 21233664 | tf_op jit(solution)/shard_map/all_to_all | solution.py:107
  (22 shorter events, 0.0 us)
Async XLA Ops:
  7.2 121.9 %all-gather.2.cloned.1.call-start = ((), (), s32[]{:S(2)}) async-start(), calls=%async_computation.2 | async-start | bytes 5898240 | tf_op jit(solution)/shard_map/all_gather | solution.py:71
  27.8 9.3 %copy-start.5 = (f32[2,1]{0,1:T(1,128)S(1)}, f32[2,1]{0,1:T(1,128)}, u32[]{:S(2)}) copy-start(f32[2,1]{0,1:T(1,128)} %param.10) | copy-start | bytes 28
  36.7 99.8 %copy-start.2 = (f32[2,1,576,256]{3,2,1,0:T(8,128)S(1)}, f32[2,1,576,256]{3,2,1,0:T(8,128)}, u32[]{:S(2)}) copy-start(f32[2,1,576,256]{3,2,1,0:T(8,128)} %bitcast_select_fusion) | copy-start | bytes 3538948
  36.8 337.6 %all-reduce.3.cloned.1.call-start = ((), (), s32[]{:S(2)}) async-start(), calls=%async_computation.3 | async-start | bytes 9437184 | tf_op jit(solution)/shard_map/psum | solution.py:90
  129.0 29.2 %slice-start = ((s8[10616832]{0:T(1024)(128)(4,1)}), s8[4194304]{0:T(1024)(128)(4,1)S(1)}, s32[]{:S(2)}) async-start(s8[10616832]{0:T(1024)(128)(4,1)} %bitcast.237), calls=%async_computation.4 | async-start | bytes 8388608
  129.0 29.2 %slice-start.6 = ((s8[4718592]{0:T(1024)(128)(4,1)}), s8[4194304]{0:T(1024)(128)(4,1)S(1)}, s32[]{:S(2)}) async-start(s8[4718592]{0:T(1024)(128)(4,1)} %bitcast.248), calls=%async_computation.10 | async-start | bytes 8388608
  136.5 21.7 %slice-start.1 = ((s8[10616832]{0:T(1024)(128)(4,1)}), s8[4194304]{0:T(1024)(128)(4,1)S(1)}, s32[]{:S(2)}) async-start(s8[10616832]{0:T(1024)(128)(4,1)} %bitcast.237), calls=%async_computation.5 | async-start | bytes 8388608
  136.5 21.7 %slice-start.2 = ((s8[10616832]{0:T(1024)(128)(4,1)}), s8[2228224]{0:T(1024)(128)(4,1)S(1)}, s32[]{:S(2)}) async-start(s8[10616832]{0:T(1024)(128)(4,1)} %bitcast.237), calls=%async_computation.6 | async-start | bytes 4456448
  136.5 21.7 %slice-start.7 = ((s8[4718592]{0:T(1024)(128)(4,1)}), s8[524288]{0:T(1024)(128)(4,1)S(1)}, s32[]{:S(2)}) async-start(s8[4718592]{0:T(1024)(128)(4,1)} %bitcast.248), calls=%async_computation.11 | async-start | bytes 1048576
  158.2 4.4 copy-start.3
  203.8 187.7 %slice-start.3 = ((s8[10616832]{0:T(1024)(128)(4,1)}), s8[2228224]{0:T(1024)(128)(4,1)S(1)}, s32[]{:S(2)}) async-start(s8[10616832]{0:T(1024)(128)(4,1)} %bitcast.239), calls=%async_computation.7 | async-start | bytes 4456448
  374.4 10.2 %copy-start = (f32[2304,2,1,256]{3,0,2,1:T(8,128)S(1)}, f32[2304,2,1,256]{3,0,2,1:T(8,128)}, u32[]{:S(2)}) copy-start(f32[2304,2,1,256]{3,0,2,1:T(8,128)} %all-reduce.3.cloned.1.call-done) | copy-start | bytes 14155780
  376.7 20.5 %copy-start.1 = (f32[2,1,576,256]{3,2,1,0:T(8,128)}, f32[2,1,576,256]{3,2,1,0:T(8,128)S(1)}, u32[]{:S(2)}) copy-start(f32[2,1,576,256]{3,2,1,0:T(8,128)S(1)} %get-tuple-element.9) | copy-start | bytes 3538948
  376.7 14.8 %slice-start.4 = ((s8[10616832]{0:T(1024)(128)(4,1)}), s8[4194304]{0:T(1024)(128)(4,1)S(1)}, s32[]{:S(2)}) async-start(s8[10616832]{0:T(1024)(128)(4,1)} %bitcast.239), calls=%async_computation.8 | async-start | bytes 8388608
  384.5 7.0 slice-start.5
  501.5 5.3 copy-start.4
  501.5 123.2 %all-to-all-start = ((f32[2,1,576,2304]{3,0,1,2:T(2,128)}), f32[2,1,576,2304]{3,0,1,2:T(2,128)}, u32[]{:S(2)}, u32[]{:S(2)}) async-start(f32[2,1,576,2304]{3,0,1,2:T(2,128)} %copy.37), calls=%async_computation | async-start | bytes 21233664 | tf_op jit(solution)/shard_map/all_to_all | solution.py:105
  712.2 123.1 %all-to-all-start.1 = ((f32[2,8,72,2304]{3,2,0,1:T(8,128)}), f32[2,8,72,2304]{3,2,0,1:T(8,128)}, u32[]{:S(2)}, u32[]{:S(2)}) async-start(f32[2,8,72,2304]{3,2,0,1:T(8,128)} %copy.44), calls=%async_computation.1 | async-start | bytes 21233664 | tf_op jit(solution)/shard_map/all_to_all | solution.py:107
Sparse Core Ops, SparseCore 0:
  36.9 92.0 all-gather.1
  203.9 170.3 all-reduce.2
where the time goes:
time: 856 us; the launch traced here: 851 us
  waiting for transfers between devices  496 us (58%)
  matrix products  157 us (18%)
  local copies, waits for them, and re-layouts  81.3 us (9%)
  other arithmetic  50.4 us (6%)
  blocking collectives  39.4 us (5%)
  between operations  16.6 us (2%)
  starting transfers between devices  10.8 us (1%)
    psum x1, waiting for transfers between devices, on_device(): summed_all = lax.psum(summed_terms, 'rcv')  171 us
    all_to_all x1, waiting for transfers between devices, on_device(): lax.all_to_all(updated, 'freq', split_axis=2, concat_axis=1, tiled=True)  117 us
    all_to_all x1, waiting for transfers between devices, on_device(): lax.all_to_all(shrunk, 'freq', split_axis=1, concat_axis=2, tiled=True)  117 us
    all_gather x1, waiting for transfers between devices, on_device(): shard_piece = lax.all_gather(picked, 'rcv', axis=2, tiled=True)  91.2 us
    psum x1, blocking collectives, on_device(): totals = lax.psum((norm_dir, norm_img), ('freq', 'rcv'))  39.4 us
    scatter-add x1, other arithmetic, on_device(): updated = green_freq.at[:, :, :, sources].add(step_size * direction)  31 us
    scatter-add x1, local copies, waits for them, and re-layouts, on_device(): updated = green_freq.at[:, :, :, sources].add(step_size * direction)  21.2 us
    unnamed x31, local copies, waits for them, and re-layouts  20 us
  transfers between devices with their start and end apart: 4, of which 4 were waited for; matrix products, arithmetic and copies ran while one was open for 0% of the time, Pallas kernels for 0%

commit v1 on v0

--- a/solution.py
+++ b/solution.py
@@ -5,6 +5,17 @@
 from jax.sharding import PartitionSpec as P
 
 HIGHEST = lax.Precision.HIGHEST
+
+
+def around_the_ring(array, mesh_axis, dim):
+    size = lax.axis_size(mesh_axis)
+    right = [(i, (i + 1) % size) for i in range(size)]
+    terms = [array]
+    for far in range(1, size):
+        terms = [lax.ppermute(terms[0], mesh_axis, right), *terms]
+    full = jnp.concatenate(terms, axis=dim)
+    offset = (lax.axis_index(mesh_axis) + 1) * terms[-1].shape[dim]
+    return jnp.roll(full, offset, axis=dim)
 
 
 def complex_product(left_pair, right_pair, pattern):
@@ -68,7 +79,7 @@
     wave_real = wavelet[0][:, None, None]
     wave_imag = wavelet[1][:, None, None]
     rows_here = green_freq.shape[2]
-    shard_piece = lax.all_gather(picked, "rcv", axis=2, tiled=True)
+    shard_piece = around_the_ring(picked, "rcv", 2)
     block_real = data_matrix[0]
     block_imag = data_matrix[1]
     real_part, imag_part = complex_product(

time: 856 us -> 851 us (level)
    all_gather x1 -> x0, waiting for transfers between devices: 91.2 us -> none  [on_device(): shard_piece = lax.all_gather(picked, 'rcv', axis=2, tiled=True)]
    ppermute x0 -> x3, waiting for transfers between devices: none -> 84.8 us  [around_the_ring(): terms = [lax.ppermute(terms[0], mesh_axis, right), *terms]]
    unnamed x31 -> x39, local copies, waits for them, and re-layouts: 20 us -> 26.9 us
  transfers between devices with their start and end apart: 4 -> 6, of which waited for: 4 -> 6; matrix products, arithmetic and copies ran while one was open for 0% -> 0% of each run, Pallas kernels for 0% -> 0%
where the time goes in v1:
time: 851 us; the launch traced here: 845 us
  waiting for transfers between devices  489 us (57%)
  matrix products  149 us (18%)
  local copies, waits for them, and re-layouts  87.5 us (10%)
  other arithmetic  49.6 us (6%)
  blocking collectives  39.4 us (5%)
  between operations  16.8 us (2%)
  starting transfers between devices  14.1 us (2%)
    psum x1, waiting for transfers between devices, on_device(): summed_all = lax.psum(summed_terms, 'rcv')  170 us
    all_to_all x1, waiting for transfers between devices, on_device(): lax.all_to_all(updated, 'freq', split_axis=2, concat_axis=1, tiled=True)  117 us
    all_to_all x1, waiting for transfers between devices, on_device(): lax.all_to_all(shrunk, 'freq', split_axis=1, concat_axis=2, tiled=True)  117 us
    ppermute x3, waiting for transfers between devices, around_the_ring(): terms = [lax.ppermute(terms[0], mesh_axis, right), *terms]  84.8 us
    psum x1, blocking collectives, on_device(): totals = lax.psum((norm_dir, norm_img), ('freq', 'rcv'))  39.4 us
    scatter-add x1, other arithmetic, on_device(): updated = green_freq.at[:, :, :, sources].add(step_size * direction)  31 us
    unnamed x39, local copies, waits for them, and re-layouts  26.9 us
    scatter-add x1, local copies, waits for them, and re-layouts, on_device(): updated = green_freq.at[:, :, :, sources].add(step_size * direction)  21.2 us
  transfers between devices with their start and end apart: 6, of which 6 were waited for; matrix products, arithmetic and copies ran while one was open for 0% of the time, Pallas kernels for 0%

profile of v1, /device:TPU:0, one launch (start us, length us, event | category | flops | bytes accessed | tf_op | source)
XLA Modules:
  0.0 845.3 jit_solution(4104606612418833740)
XLA Ops:
  7.2 0.0 all-reduce.3.cloned.1.call-start
  7.2 0.7 compare_select_fusion
  7.9 0.7 compare_and_fusion
  8.6 19.2 %copy.30 = f32[2,1,576,2304]{2,0,3,1:T(2,128)} copy(f32[2,1,576,2304]{3,2,1,0:T(8,128)} %param.7) | data formatting | bytes 21233664 | tf_op args[0]
  27.8 6.5 gather_fusion
  34.4 1.2 copy.31
  35.6 0.1 bitcast_select_fusion
  35.7 3.1 collective-permute-start
  38.8 28.0 %collective-permute-done = f32[2,1,576,256]{3,2,1,0:T(8,128)S(1)} collective-permute-done((f32[2,1,576,256]{3,2,1,0:T(8,128)S(1)}, f32[2,1,576,256]{3,2,1,0:T(8,128)S(1)}, u32[]{:S(2)}, u32[]{:S(2)}) %collective-permute-start) | collective-permute-done | bytes 1179680 | tf_op jit(solution)/shard_map/ppermute | solution.py:15
  66.8 1.0 copy-done.2
  67.9 29.0 %collective-permute-done.1 = f32[2,1,576,256]{3,2,1,0:T(8,128)} collective-permute-done((f32[2,1,576,256]{3,2,1,0:T(8,128)S(1)}, f32[2,1,576,256]{3,2,1,0:T(8,128)}, u32[]{:S(2)}, u32[]{:S(2)}) %collective-permute-start.1) | collective-permute-done | bytes 1179680 | tf_op jit(solution)/shard_map/ppermute | solution.py:15
  96.9 0.5 collective-permute-start.2
  97.5 0.6 fusion.179
  98.0 27.7 %collective-permute-done.2 = f32[2,1,576,256]{3,2,1,0:T(8,128)} collective-permute-done((f32[2,1,576,256]{3,2,1,0:T(8,128)}, f32[2,1,576,256]{3,2,1,0:T(8,128)}, u32[]{:S(2)}, u32[]{:S(2)}) %collective-permute-start.2) | collective-permute-done | bytes 1179680 | tf_op jit(solution)/shard_map/ppermute | solution.py:15
  125.8 1.3 constant_dynamic-update-slice_fusion.7
  127.1 1.5 constant_dynamic-update-slice_fusion.6
  128.7 0.1 constant_dynamic-update-slice_fusion.5
  128.7 0.1 constant_dynamic-update-slice_fusion.4
  128.9 1.5 constant_dynamic-update-slice_fusion.3
  130.4 1.4 constant_dynamic-update-slice_fusion.2
  131.8 0.1 constant_dynamic-update-slice_fusion.1
  131.8 0.1 constant_dynamic-update-slice_fusion
  132.0 4.4 fusion.8
  136.4 4.4 fusion.10
  140.8 5.8 fusion.101
  146.6 5.6 fusion.98
  152.3 10.3 %fusion.6 = f32[256,2304]{0,1:T(8,128)S(1)} fusion(f32[576,256]{1,0:T(8,128)S(1)} %fusion.101, f32[2,1,576,2304]{3,2,1,0:T(8,128)S(1)} %bitcast.242), kind=kOutput, calls=%fused_computation.9 | convolution fusion | flops 4076863488 | bytes 8257536 | tf_op jit(solution)/shard_map/frk,frc->kfc/dot_general | solution.py:36
  162.5 1.4 add_bitcast_fusion
  163.9 10.5 %fusion.4 = f32[256,2304]{0,1:T(8,128)S(1)} fusion(f32[576,256]{1,0:T(8,128)S(1)} %fusion.98, f32[2,1,576,2304]{3,2,1,0:T(8,128)S(1)} %bitcast.242), kind=kOutput, calls=%fused_computation.7 | convolution fusion | flops 4076863488 | bytes 8257536 | tf_op jit(solution)/shard_map/frk,frc->kfc/dot_general | solution.py:39
  174.4 9.5 %fusion.41 = f32[2304,1,1,256]{3,0,2,1:T(8,128)S(1)} fusion(f32[256,2304]{0,1:T(8,128)S(1)} %fusion.6, f32[576,256]{1,0:T(8,128)S(1)} %fusion.98, f32[2,1,576,2304]{3,2,1,0:T(8,128)S(1)} %bitcast.242), kind=kOutput, calls=%fused_computation.44 | convolution fusion | flops 4077453312 | bytes 10616832 | tf_op jit(solution)/shard_map/frk,frc->kfc/dot_general | solution.py:36
  184.0 9.7 %fusion.38 = f32[2304,1,1,256]{3,0,2,1:T(8,128)S(1)} fusion(f32[256,2304]{0,1:T(8,128)S(1)} %fusion.4, f32[576,256]{1,0:T(8,128)S(1)} %fusion.101, f32[2,1,576,2304]{3,2,1,0:T(8,128)S(1)} %bitcast.242), kind=kOutput, calls=%fused_computation.43 | convolution fusion | flops 4077453312 | bytes 10616832 | tf_op jit(solution)/shard_map/frk,frc->kfc/dot_general | solution.py:39
  193.7 2.5 maximum_negate_fusion
  196.2 2.4 fusion.108
  198.6 0.0 all-reduce.3.cloned.1.call-update
  198.7 169.9 %all-reduce.3.cloned.1.call-done = f32[2304,2,1,256]{3,0,2,1:T(8,128)} async-done(((f32[2304,2,1,256]{3,0,2,1:T(8,128)}), f32[2304,2,1,256]{3,0,2,1:T(8,128)}) %all-reduce.3.cloned.1.call-update) | async-done | bytes 4718608 | tf_op jit(solution)/shard_map/psum | solution.py:101
  368.5 2.3 multiply_reduce_fusion
  370.9 7.8 fusion
  378.7 7.2 fusion.2
  386.0 5.6 fusion.83
  391.6 6.3 fusion.109
  397.9 39.4 %all-reduce = (f32[]{:T(128)}, f32[]{:T(128)}) all-reduce(f32[]{:T(128)} %get-tuple-element.8, f32[]{:T(128)} %fusion.109), channel_id=1, replica_groups=mesh['freq'=8,'rcv'=4] {'freq','rcv'}, use_global_device_ids=true, to_apply=%region_2.3 | all-reduce | flops 2 | bytes 16 | tf_op jit(solution)/shard_map/psum | solution.py:112
  438.7 2.4 multiply_bitcast_fusion.2
  441.1 2.7 copy.36
  443.7 31.0 %scatter_fusion = f32[2,576,2304]{1,0,2:T(2,128)} fusion(f32[2,576,2304]{1,0,2:T(2,128)} %bitcast.246, s32[256]{0:T(256)S(1)} %compare_select_fusion, f32[256,2,576]{2,1,0:T(2,128)S(1)} %copy.36), kind=kCustom, calls=%fused_computation.1 | custom fusion | flops 294912 | bytes 3539968 | tf_op jit(solution)/shard_map/scatter-add | solution.py:114
  474.8 21.2 %copy.37 = f32[2,1,576,2304]{3,0,1,2:T(2,128)} copy(f32[2,1,576,2304]{2,0,3,1:T(2,128)} %bitcast.247) | data formatting | bytes 21233664 | tf_op jit(solution)/shard_map/scatter-add | solution.py:114
  496.0 5.3 all-to-all-start
  501.9 117.2 %all-to-all-done = f32[2,1,576,2304]{3,0,1,2:T(2,128)} async-done(((f32[2,1,576,2304]{3,0,1,2:T(2,128)}), f32[2,1,576,2304]{3,0,1,2:T(2,128)}, u32[]{:S(2)}, u32[]{:S(2)}) %all-to-all-start) | async-done | bytes 10616864 | tf_op jit(solution)/shard_map/all_to_all | solution.py:116
  619.2 12.0 %fusion.178 = (f32[1,1,576,2304]{3,0,1,2:T(1,128)S(1)}, f32[1,1,576,2304]{3,0,1,2:T(1,128)S(1)}) fusion(f32[2,1,576,2304]{3,0,1,2:T(2,128)} %all-to-all-done), kind=kLoop, calls=%fused_computation.157 | loop fusion | bytes 21233664 | tf_op jit(solution)/shard_map/slice | solution.py:54
  631.2 0.3 copy.51
  631.5 7.0 fusion.30
  638.5 7.1 fusion.28
  645.6 0.3 copy.52
  646.0 7.1 convolution_subtract_fusion
  653.1 7.6 convolution_add_fusion
  660.7 7.6 fusion.121
  668.3 7.8 fusion.119
  676.1 8.9 %multiply_bitcast_fusion.1 = f32[1,8,72,2304]{3,1,2,0:T(8,128)} fusion(f32[8,72,2304]{2,0,1:T(8,128)S(1)} %fusion.121, f32[8,72,2304]{2,0,1:T(8,128)S(1)} %convolution_add_fusion, f32[8,72,2304]{2,0,1:T(8,128)S(1)} %convolution_subtract_fusion, f32[8,2304]{1,0:T(8,128)S(1)} %convert_element_type.21, f32[]{:T(128)} %bitcast.238), kind=kOutput, calls=%fused_computation.28 | convolution fusion | flops 142001024 | bytes 21307396 | tf_op jit(solution)/shard_map/tf,f...->t.../dot_general | solution.py:67
  685.0 9.0 %multiply_bitcast_fusion = f32[1,8,72,2304]{3,1,2,0:T(8,128)} fusion(f32[8,72,2304]{2,0,1:T(8,128)S(1)} %fusion.119, f32[8,72,2304]{2,0,1:T(8,128)S(1)} %convolution_subtract_fusion, f32[8,72,2304]{2,0,1:T(8,128)S(1)} %convolution_add_fusion, f32[8,2304]{1,0:T(8,128)S(1)} %convert_element_type.21, f32[]{:T(128)} %bitcast.239), kind=kOutput, calls=%fused_computation.27 | convolution fusion | flops 142001024 | bytes 21307396 | tf_op jit(solution)/shard_map/tf,f...->t.../dot_general | solution.py:71
  694.0 4.8 pad_maximum_fusion
  698.8 7.4 copy.44
  706.1 5.2 all-to-all-start.1
  711.3 1.1 pad_maximum_fusion.1
  712.4 116.8 %all-to-all-done.1 = f32[2,8,72,2304]{3,2,0,1:T(8,128)} async-done(((f32[2,8,72,2304]{3,2,0,1:T(8,128)}), f32[2,8,72,2304]{3,2,0,1:T(8,128)}, u32[]{:S(2)}, u32[]{:S(2)}) %all-to-all-start.1) | async-done | bytes 10616864 | tf_op jit(solution)/shard_map/all_to_all | solution.py:118
  829.2 9.0 %copy.45 = f32[2,8,72,2304]{3,2,1,0:T(8,128)} copy(f32[2,8,72,2304]{3,2,0,1:T(8,128)} %all-to-all-done.1) | data formatting | bytes 21233664 | tf_op jit(solution)/shard_map/all_to_all | solution.py:118
  (34 shorter events, 0.1 us)
Async XLA Ops:
  7.2 361.4 %all-reduce.3.cloned.1.call-start = ((), (), s32[]{:S(2)}) async-start(), calls=%async_computation.2 | async-start | bytes 9437184 | tf_op jit(solution)/shard_map/psum | solution.py:101
  27.8 69.6 %copy-start.8 = (f32[2,1]{0,1:T(1,128)S(1)}, f32[2,1]{0,1:T(1,128)}, u32[]{:S(2)}) copy-start(f32[2,1]{0,1:T(1,128)} %param.10) | copy-start | bytes 28
  35.6 96.3 %slice-start = ((s8[10616832]{0:T(1024)(128)(4,1)}), s8[2228224]{0:T(1024)(128)(4,1)S(1)}, s32[]{:S(2)}) async-start(s8[10616832]{0:T(1024)(128)(4,1)} %bitcast.241), calls=%async_computation.3 | async-start | bytes 4456448
  35.7 61.2 %copy-start.4 = (f32[2,1,576,256]{3,2,1,0:T(8,128)}, f32[2,1,576,256]{3,2,1,0:T(8,128)S(1)}, u32[]{:S(2)}) copy-start(f32[2,1,576,256]{3,2,1,0:T(8,128)S(1)} %bitcast_select_fusion) | copy-start | bytes 3538948
  35.7 31.1 %collective-permute-start = (f32[2,1,576,256]{3,2,1,0:T(8,128)S(1)}, f32[2,1,576,256]{3,2,1,0:T(8,128)S(1)}, u32[]{:S(2)}, u32[]{:S(2)}) collective-permute-start(f32[2,1,576,256]{3,2,1,0:T(8,128)S(1)} %bitcast_select_fusion), channel_id=1, source_target_pairs={{0,1},{1,2},{2,3},{3,0},{4,5},{5,6},{6,7},{7,4},{8,9},{9,10},{10,1... | collective-permute-start | bytes 3538952 | tf_op jit(solution)/shard_map/ppermute | solution.py:15
  66.8 1.0 copy-start.2
  67.8 29.0 %collective-permute-start.1 = (f32[2,1,576,256]{3,2,1,0:T(8,128)S(1)}, f32[2,1,576,256]{3,2,1,0:T(8,128)}, u32[]{:S(2)}, u32[]{:S(2)}) collective-permute-start(f32[2,1,576,256]{3,2,1,0:T(8,128)S(1)} %collective-permute-done), channel_id=1, source_target_pairs={{0,1},{1,2},{2,3},{3,0},{4,5},{5,6},{6,7},{7,4},{8,9},{9,10},{10,1... | collective-permute-start | bytes 3538952 | tf_op jit(solution)/shard_map/ppermute | solution.py:15
  96.9 28.9 %collective-permute-start.2 = (f32[2,1,576,256]{3,2,1,0:T(8,128)}, f32[2,1,576,256]{3,2,1,0:T(8,128)}, u32[]{:S(2)}, u32[]{:S(2)}) collective-permute-start(f32[2,1,576,256]{3,2,1,0:T(8,128)} %collective-permute-done.1), channel_id=1, source_target_pairs={{0,1},{1,2},{2,3},{3,0},{4,5},{5,6},{6,7},{7,4},{8,9},{9,10},{10,1... | collective-permute-start | bytes 3538952 | tf_op jit(solution)/shard_map/ppermute | solution.py:15
  97.4 31.2 %copy-start.3 = (f32[2,1,576,256]{3,2,1,0:T(8,128)S(1)}, f32[2,1,576,256]{3,2,1,0:T(8,128)}, u32[]{:S(2)}) copy-start(f32[2,1,576,256]{3,2,1,0:T(8,128)} %copy-done.2) | copy-start | bytes 3538948
  127.1 4.8 slice-start.1
  128.9 3.1 slice-start.2
  136.4 4.4 copy-start.5
  136.4 4.4 copy-start.6
  198.6 187.3 %slice-start.3 = ((s8[10616832]{0:T(1024)(128)(4,1)}), s8[2228224]{0:T(1024)(128)(4,1)S(1)}, s32[]{:S(2)}) async-start(s8[10616832]{0:T(1024)(128)(4,1)} %bitcast.243), calls=%async_computation.6 | async-start | bytes 4456448
  368.5 10.2 %copy-start = (f32[2304,2,1,256]{3,0,2,1:T(8,128)S(1)}, f32[2304,2,1,256]{3,0,2,1:T(8,128)}, u32[]{:S(2)}) copy-start(f32[2304,2,1,256]{3,0,2,1:T(8,128)} %all-reduce.3.cloned.1.call-done) | copy-start | bytes 14155780
  370.9 20.7 %copy-start.1 = (f32[2,1,576,256]{3,2,1,0:T(8,128)}, f32[2,1,576,256]{3,2,1,0:T(8,128)S(1)}, u32[]{:S(2)}) copy-start(f32[2,1,576,256]{3,2,1,0:T(8,128)S(1)} %get-tuple-element.9) | copy-start | bytes 3538948
  370.9 15.1 %slice-start.4 = ((s8[10616832]{0:T(1024)(128)(4,1)}), s8[4194304]{0:T(1024)(128)(4,1)S(1)}, s32[]{:S(2)}) async-start(s8[10616832]{0:T(1024)(128)(4,1)} %bitcast.243), calls=%async_computation.7 | async-start | bytes 8388608
  378.7 7.2 slice-start.5
  496.0 5.3 copy-start.7
  496.0 123.2 %all-to-all-start = ((f32[2,1,576,2304]{3,0,1,2:T(2,128)}), f32[2,1,576,2304]{3,0,1,2:T(2,128)}, u32[]{:S(2)}, u32[]{:S(2)}) async-start(f32[2,1,576,2304]{3,0,1,2:T(2,128)} %copy.37), calls=%async_computation | async-start | bytes 21233664 | tf_op jit(solution)/shard_map/all_to_all | solution.py:116
  706.1 123.1 %all-to-all-start.1 = ((f32[2,8,72,2304]{3,2,0,1:T(8,128)}), f32[2,8,72,2304]{3,2,0,1:T(8,128)}, u32[]{:S(2)}, u32[]{:S(2)}) async-start(f32[2,8,72,2304]{3,2,0,1:T(8,128)} %copy.44), calls=%async_computation.1 | async-start | bytes 21233664 | tf_op jit(solution)/shard_map/all_to_all | solution.py:118
Sparse Core Ops, SparseCore 0:
  198.8 169.7 all-reduce.2
